TPU v7x, 32 devices: a whole 2x2x4 slice. The times are simulated.
32 devices in a mesh: groups: 2 (over y), expert: 4 (over z), dp: 4 (over x, core).
Axes of the slice: x: 2, y: 2, z: 4, core: 2. Of those that a mesh axis runs over, the one named last changes fastest.
Arguments:
- tokens: bfloat16 [4096, 1280], P(('groups', 'expert', 'dp')), parts along dimension 0, may hold values from -6 to 6
- cotangent: bfloat16 [4096, 1280], P(('groups', 'expert', 'dp')), parts along dimension 0, may hold values from -3 to 3
- expert_ids: int32 [4096, 6], P(('groups', 'expert', 'dp')), parts along dimension 0, may hold values from 0 to 15, all different within a row; in each aligned block of 128 rows (0 to 127, 128 to 255, ...) at most 52 rows name the same one
- gate_values: bfloat16 [4096, 6], P(('groups', 'expert', 'dp')), parts along dimension 0, may hold values from 0.099609375 to 1
- gate_weight: bfloat16 [16, 1280, 768], P('expert'), may hold values from -0.15625 to 0.15625
- up_weight: bfloat16 [16, 1280, 768], P('expert'), may hold values from -0.15625 to 0.15625
- down_weight: bfloat16 [16, 768, 1280], P('expert'), may hold values from -0.21875 to 0.21875
Outputs:
- layer_out: bfloat16 [4096, 1280], P(('groups', 'expert', 'dp')), parts along dimension 0
- grad_tokens: bfloat16 [4096, 1280], P(('groups', 'expert', 'dp')), parts along dimension 0
- grad_gate: float32 [32, 1280, 768], P(('groups', 'expert'), 'dp'), parts along dimension 0
- grad_up: float32 [32, 1280, 768], P(('groups', 'expert'), 'dp'), parts along dimension 0
- grad_down: float32 [32, 768, 1280], P(('groups', 'expert'), 'dp'), parts along dimension 0
There are 2 independent parts, one for each index of `groups`. A program takes and returns all parts, laid end to end along the dimension named above; an argument that names none is the same for every part. Nothing has to cross between parts.
Inputs may be any that keep to these rules, and one draw needn't show every extreme that they name: `expert_ids`: each row names 6 different experts. Among the 128 rows of one device (aligned blocks of rows), no expert is named by more than 52 rows, and in some blocks an expert is named by exactly 52 rows.
All inputs are finite; a program needn't handle non-finite values.
Results may differ from a plain program's by a relative error of at most 0.015.
Values may be sent and summed in bfloat16 or wider, within the bound.
A program may use at most 128 MiB of HBM per device.

v0:
```python
import jax
import jax.numpy as jnp
from jax import lax
from jax.sharding import PartitionSpec as P


def expert_forward(inputs, gate_weight, up_weight, down_weight):
    gate_sums = jnp.einsum("erd,edf->erf", inputs, gate_weight, preferred_element_type=jnp.float32)
    up_sums = jnp.einsum("erd,edf->erf", inputs, up_weight, preferred_element_type=jnp.float32)
    hidden = (jax.nn.silu(gate_sums) * up_sums).astype(jnp.bfloat16)
    expert_out = jnp.einsum(
        "erf,efd->erd", hidden, down_weight, preferred_element_type=jnp.float32
    ).astype(jnp.bfloat16)
    return ((gate_sums, up_sums, hidden), expert_out)


def expert_backward(inputs, out_grad, saved_state, gate_weight, up_weight, down_weight):
    gate_sums, up_sums, hidden = saved_state
    hidden_grad = jnp.einsum(
        "erd,efd->erf", out_grad, down_weight, preferred_element_type=jnp.float32
    )
    sigmoid = jax.nn.sigmoid(gate_sums)
    gate_back = (hidden_grad * up_sums * sigmoid * (1.0 + gate_sums * (1.0 - sigmoid))).astype(
        jnp.bfloat16
    )
    up_back = (hidden_grad * (gate_sums * sigmoid)).astype(jnp.bfloat16)
    slot_grad = jnp.einsum(
        "erf,edf->erd", gate_back, gate_weight, preferred_element_type=jnp.float32
    )
    slot_grad = (
        slot_grad
        + jnp.einsum("erf,edf->erd", up_back, up_weight, preferred_element_type=jnp.float32)
    ).astype(jnp.bfloat16)
    part_gate = jnp.einsum(
        "erd,erf->edf", inputs, gate_back, preferred_element_type=jnp.float32
    ).astype(jnp.bfloat16)
    part_up = jnp.einsum(
        "erd,erf->edf", inputs, up_back, preferred_element_type=jnp.float32
    ).astype(jnp.bfloat16)
    part_down = jnp.einsum(
        "erf,erd->efd", hidden, out_grad, preferred_element_type=jnp.float32
    ).astype(jnp.bfloat16)
    return (slot_grad, part_gate, part_up, part_down)


def shards(tokens, cotangent, expert_ids, gate_values, gate_weight, up_weight, down_weight):
    tok_rows, model_width = tokens.shape
    top_count = expert_ids.shape[1]
    exp_local = gate_weight.shape[0]
    peer_count = lax.axis_size("expert")
    experts = exp_local * peer_count
    slot_count = tok_rows * top_count
    capacity = (slot_count + slot_count // 12) // experts
    bf_zero = jnp.zeros((), jnp.bfloat16)
    flat_ids = expert_ids.reshape(slot_count)
    onehot = (flat_ids[:, None] == jnp.arange(experts, dtype=jnp.int32)[None, :]).astype(jnp.int32)
    slot_rank = jnp.sum((jnp.cumsum(onehot, axis=0) - 1) * onehot, axis=1)
    slot_dest = flat_ids * capacity + slot_rank
    slot_owner = (
        jnp.full((experts * capacity,), slot_count, jnp.int32)
        .at[slot_dest]
        .set(jnp.arange(slot_count, dtype=jnp.int32))
    )
    filled = slot_owner < slot_count
    owner_safe = jnp.where(filled, slot_owner, 0)
    source_row = owner_safe // top_count
    slot_gate = jnp.where(
        filled, jnp.take(gate_values.reshape(slot_count), owner_safe).astype(jnp.float32), 0.0
    )
    sent_tokens = jnp.where(filled[:, None], jnp.take(tokens, source_row, axis=0), bf_zero).reshape(
        experts, capacity, model_width
    )
    sent_grads = (
        slot_gate[:, None] * jnp.take(cotangent, source_row, axis=0).astype(jnp.float32)
    ).astype(jnp.bfloat16)
    sent_grads = sent_grads.reshape(experts, capacity, model_width)
    arrived = lax.all_to_all(sent_tokens, "expert", split_axis=0, concat_axis=1, tiled=True)
    saved_state, expert_out = expert_forward(arrived, gate_weight, up_weight, down_weight)
    returned = lax.all_to_all(expert_out, "expert", split_axis=1, concat_axis=0, tiled=True)
    arrived_grads = lax.all_to_all(sent_grads, "expert", split_axis=0, concat_axis=1, tiled=True)
    slot_grad, part_gate, part_up, part_down = expert_backward(
        arrived, arrived_grads, saved_state, gate_weight, up_weight, down_weight
    )
    returned_grads = lax.all_to_all(slot_grad, "expert", split_axis=1, concat_axis=0, tiled=True)

    def collect(returned_rows):
        picked = jnp.take(returned_rows.reshape(experts * capacity, model_width), slot_dest, axis=0)
        return picked.reshape(tok_rows, top_count, model_width).astype(jnp.float32)

    layer_out = jnp.sum(
        gate_values.astype(jnp.float32)[:, :, None] * collect(returned), axis=1
    ).astype(jnp.bfloat16)
    grad_tokens = jnp.sum(collect(returned_grads), axis=1).astype(jnp.bfloat16)
    grad_gate, grad_up, grad_down = (
        lax.psum_scatter(part_gate, "dp", scatter_dimension=1, tiled=True).astype(jnp.float32),
        lax.psum_scatter(part_up, "dp", scatter_dimension=1, tiled=True).astype(jnp.float32),
        lax.psum_scatter(part_down, "dp", scatter_dimension=1, tiled=True).astype(jnp.float32),
    )
    return (layer_out, grad_tokens, grad_gate, grad_up, grad_down)


def solution(mesh):
    return jax.shard_map(
        shards,
        mesh=mesh,
        in_specs=(
            P(("groups", "expert", "dp"), None),
            P(("groups", "expert", "dp"), None),
            P(("groups", "expert", "dp"), None),
            P(("groups", "expert", "dp"), None),
            P("expert", None, None),
            P("expert", None, None),
            P("expert", None, None),
        ),
        out_specs=(
            P(("groups", "expert", "dp"), None),
            P(("groups", "expert", "dp"), None),
            P(("groups", "expert"), "dp", None),
            P(("groups", "expert"), "dp", None),
            P(("groups", "expert"), "dp", None),
        ),
        check_vma=False,
    )
```

profile of v0, /device:TPU:0, one launch (start us, length us, event | category | flops | bytes accessed | tf_op | source)
XLA Modules:
  0.0 390.8 jit_solution(152963916954298211)
XLA Ops:
  11.4 3.4 scatter_custom_fusion
  15.8 5.4 %gather_fusion = bf16[832]{0:T(1024)(128)(2,1)S(1)} fusion(bf16[768]{0:T(1024)(128)(2,1)S(1)} %reshape.102, s32[1024]{0:T(1024)S(1)} %pad_clamp_fusion), kind=kCustom, calls=%fused_computation.4 | custom fusion | bytes 6656 | tf_op jit(solution)/shard_map/jit(_take)/gather | solution.py:68
  21.3 4.3 %gather_fusion.3 = bf16[832,1280]{1,0:T(8,128)(2,1)} fusion(bf16[128,1280]{1,0:T(8,128)(2,1)S(1)} %copy-done, s32[1024]{0:T(1024)S(1)} %pad_clamp_fusion.2), kind=kCustom, calls=%fused_computation.2.clone | custom fusion | bytes 4263168 | tf_op jit(solution)/shard_map/jit(_take)/gather | solution.py:74
  29.8 6.4 %all-to-all-start.2 = ((bf16[16,52,1280]{2,1,0:T(8,128)(2,1)}), bf16[16,52,1280]{2,1,0:T(8,128)(2,1)S(1)}, u32[]{:S(2)}, u32[]{:S(2)}) async-start(bf16[16,52,1280]{2,1,0:T(8,128)(2,1)} %reshape.103), calls=%async_computation.2 | async-start | bytes 4587520 | tf_op jit(solution)/shard_map/all_to_all | solution.py:80
  36.2 4.3 %gather_fusion.1 = bf16[832,1280]{1,0:T(8,128)(2,1)} fusion(bf16[128,1280]{1,0:T(8,128)(2,1)S(1)} %copy-done.2, s32[1024]{0:T(1024)S(1)} %pad_clamp_fusion.2), kind=kCustom, calls=%fused_computation.clone | custom fusion | bytes 4263168 | tf_op jit(solution)/shard_map/jit(_take)/gather | solution.py:70
  43.4 3.9 %reshape.100 = bf16[16,52,1280]{2,1,0:T(8,128)(2,1)} reshape(bf16[832,1280]{1,0:T(8,128)(2,1)} %select_select_fusion) | data formatting | bytes 4259840 | tf_op jit(solution)/shard_map/reshape | solution.py:70
  47.4 41.2 %all-to-all-done.2 = bf16[16,52,1280]{2,1,0:T(8,128)(2,1)S(1)} async-done(((bf16[16,52,1280]{2,1,0:T(8,128)(2,1)}), bf16[16,52,1280]{2,1,0:T(8,128)(2,1)S(1)}, u32[]{:S(2)}, u32[]{:S(2)}) %all-to-all-start.2) | async-done | bytes 2129952 | tf_op jit(solution)/shard_map/all_to_all | solution.py:80
  88.6 4.5 %all-to-all-start = ((bf16[16,52,1280]{2,1,0:T(8,128)(2,1)}), bf16[16,52,1280]{2,1,0:T(8,128)(2,1)}, u32[]{:S(2)}, u32[]{:S(2)}) async-start(bf16[16,52,1280]{2,1,0:T(8,128)(2,1)} %reshape.100), calls=%async_computation | async-start | bytes 4587520 | tf_op jit(solution)/shard_map/all_to_all | solution.py:77
  95.5 49.6 %all-to-all-done = bf16[16,52,1280]{2,1,0:T(8,128)(2,1)} async-done(((bf16[16,52,1280]{2,1,0:T(8,128)(2,1)}), bf16[16,52,1280]{2,1,0:T(8,128)(2,1)}, u32[]{:S(2)}, u32[]{:S(2)}) %all-to-all-start) | async-done | bytes 2129952 | tf_op jit(solution)/shard_map/all_to_all | solution.py:77
  147.7 5.2 %fusion.6 = f32[4,208,768]{2,1,0:T(8,128)S(1)} fusion(bf16[4,1280,768]{2,1,0:T(8,128)(2,1)} %param.16, bf16[4,208,1280]{2,0,1:T(4,128)(2,1)S(1)} %bitcast.44), kind=kOutput, calls=%fused_computation.26 | convolution fusion | flops 1635778560 | bytes 12550144 | tf_op jit(solution)/shard_map/erd,edf->erf/dot_general | solution.py:9
  154.8 7.7 %multiply_convert_fusion.1 = (bf16[4,208,768]{2,1,0:T(8,128)(2,1)}, bf16[4,208,768]{2,1,0:T(8,128)(2,1)}, bf16[4,208,768]{2,1,0:T(8,128)(2,1)S(1)}) fusion(f32[4,208,768]{2,1,0:T(8,128)S(1)} %fusion.8, f32[4,208,768]{2,1,0:T(8,128)S(1)} %fusion.6, bf16[4,768,1280]{2,1,0:T(8,128)(2,1)} %param.17, bf16[4,208,1280]{2,0,1:T(4,128)(2,1)S(1)} %bitcast.50), kind=kOutput, calls=%fused_computation.13 | convolution fusion | flops 1645363200 | bytes 18939904 | tf_op jit(solution)/shard_map/erd,efd->erf/dot_general | solution.py:19
  163.6 5.4 %convolution_convert_fusion = bf16[4,768,1280]{2,1,0:T(8,128)(2,1)} fusion(bf16[4,208,768]{2,1,0:T(8,128)(2,1)S(1)} %get-tuple-element.15, bf16[4,208,1280]{2,0,1:T(4,128)(2,1)S(1)} %bitcast.51), kind=kOutput, calls=%fused_computation.6 | convolution fusion | flops 1639710720 | bytes 11272192 | tf_op jit(solution)/shard_map/erf,erd->efd/dot_general | solution.py:40
  169.0 8.1 %convolution_convert_fusion.2 = bf16[4,1280,768]{2,1,0:T(8,128)(2,1)} fusion(bf16[4,208,768]{2,1,0:T(8,128)(2,1)} %get-tuple-element.14, bf16[4,208,1280]{2,0,1:T(4,128)(2,1)S(1)} %bitcast.46), kind=kOutput, calls=%fused_computation.8 | convolution fusion | flops 1639710720 | bytes 11272192 | tf_op jit(solution)/shard_map/erd,erf->edf/dot_general | solution.py:34
  177.4 7.0 %convolution_convert_fusion.1 = bf16[4,1280,768]{2,1,0:T(8,128)(2,1)} fusion(bf16[4,208,768]{2,1,0:T(8,128)(2,1)} %get-tuple-element.13, bf16[4,208,1280]{2,0,1:T(4,128)(2,1)S(1)} %bitcast.47), kind=kOutput, calls=%fused_computation.7 | convolution fusion | flops 1639710720 | bytes 11272192 | tf_op jit(solution)/shard_map/erd,erf->edf/dot_general | solution.py:37
  185.7 5.9 %fusion.17 = f32[4,208,1280]{2,1,0:T(8,128)S(1)} fusion(bf16[4,208,768]{2,1,0:T(8,128)(2,1)S(1)} %copy-done.4, bf16[4,1280,768]{2,1,0:T(8,128)(2,1)} %param.15), kind=kOutput, calls=%fused_computation.58 | convolution fusion | flops 1635778560 | bytes 13402112 | tf_op jit(solution)/shard_map/erf,edf->erd/dot_general | solution.py:27
  191.6 6.5 %add_convert_fusion = bf16[4,208,1280]{2,1,0:T(8,128)(2,1)S(1)} fusion(f32[4,208,1280]{2,1,0:T(8,128)S(1)} %fusion.17, bf16[4,208,768]{2,1,0:T(8,128)(2,1)S(1)} %copy-done.6, bf16[4,1280,768]{2,1,0:T(8,128)(2,1)} %param.16), kind=kOutput, calls=%fused_computation.10 | convolution fusion | flops 1637908480 | bytes 15532032 | tf_op jit(solution)/shard_map/erf,edf->erd/dot_general | solution.py:32
  200.4 3.6 all-to-all-start.3
  204.1 5.6 %convolution_convert_fusion.3 = bf16[4,208,1280]{2,1,0:T(8,128)(2,1)S(1)} fusion(bf16[4,208,768]{2,1,0:T(8,128)(2,1)} %copy-done.5, bf16[4,768,1280]{2,1,0:T(8,128)(2,1)} %param.17), kind=kOutput, calls=%fused_computation.12 | convolution fusion | flops 1636843520 | bytes 11272192 | tf_op jit(solution)/shard_map/erf,efd->erd/dot_general | solution.py:11
  212.1 40.7 %all-to-all-done.3 = bf16[4,208,1280]{2,0,1:T(4,128)(2,1)S(1)} async-done(((bf16[4,208,1280]{2,0,1:T(4,128)(2,1)}), bf16[4,208,1280]{2,0,1:T(4,128)(2,1)S(1)}, u32[]{:S(2)}, u32[]{:S(2)}) %all-to-all-start.3) | async-done | bytes 2129952 | tf_op jit(solution)/shard_map/all_to_all | solution.py:84
  252.8 4.8 %all-to-all-start.1 = ((bf16[4,208,1280]{2,0,1:T(4,128)(2,1)}), bf16[4,208,1280]{2,0,1:T(4,128)(2,1)}, u32[]{:S(2)}, u32[]{:S(2)}) async-start(bf16[4,208,1280]{2,0,1:T(4,128)(2,1)} %copy.44), calls=%async_computation.1 | async-start | bytes 4259840 | tf_op jit(solution)/shard_map/all_to_all | solution.py:79
  262.0 43.8 %all-to-all-done.1 = bf16[4,208,1280]{2,0,1:T(4,128)(2,1)} async-done(((bf16[4,208,1280]{2,0,1:T(4,128)(2,1)}), bf16[4,208,1280]{2,0,1:T(4,128)(2,1)}, u32[]{:S(2)}, u32[]{:S(2)}) %all-to-all-start.1) | async-done | bytes 2129952 | tf_op jit(solution)/shard_map/all_to_all | solution.py:79
  305.8 3.3 copy.45
  309.0 4.0 %reshape.101 = bf16[832,1280]{1,0:T(8,128)(2,1)} reshape(bf16[4,4,52,1280]{3,2,1,0:T(8,128)(2,1)} %copy.45) | data formatting | bytes 4259840 | tf_op jit(solution)/shard_map/reshape | solution.py:87
  313.0 3.7 gather_fusion.4
  316.7 7.7 %gather_fusion.2 = bf16[768,1280]{1,0:T(8,128)(2,1)} fusion(bf16[832,1280]{1,0:T(8,128)(2,1)} %reshape.101, s32[1024]{0:T(1024)S(1)} %pad_clamp_fusion.1), kind=kCustom, calls=%fused_computation.1.clone | custom fusion | bytes 3935232 | tf_op jit(solution)/shard_map/jit(_take)/gather | solution.py:87
  324.4 4.7 %broadcast_select_fusion = (bf16[768,1280]{1,0:T(8,128)(2,1)}, f32[768,1280]{1,0:T(8,128)}) fusion(bf16[768,1280]{1,0:T(8,128)(2,1)S(1)} %copy-done.7, pred[768]{0:T(1024)(128)(4,1)S(1)} %get-tuple-element.9, bf16[768,1280]{1,0:T(8,128)(2,1)} %gather_fusion.2), kind=kLoop, calls=%fused_computation.20 | loop fusion | flops 2949120 | bytes 9831168 | tf_op jit(solution)/shard_map/jit(_take)/select_n | solution.py:87
  329.1 5.0 %reshape.106 = f32[128,6,1280]{2,1,0:T(8,128)} reshape(f32[768,1280]{1,0:T(8,128)} %get-tuple-element.17) | data formatting | bytes 7864320 | tf_op jit(solution)/shard_map/convert_element_type | solution.py:88
  339.6 4.9 %multiply_reduce_fusion = bf16[128,1280]{1,0:T(8,128)(2,1)} fusion(f32[128,6,1280]{2,1,0:T(8,128)} %reshape.106, f32[128,6]{1,0:T(8,128)S(1)} %copy.35), kind=kLoop, calls=%fused_computation.9 | loop fusion | flops 1802240 | bytes 4262912 | tf_op jit(solution)/shard_map/reduce_sum | solution.py:90
  344.4 3.8 convert_element_type.79
  348.2 3.9 %convert_element_type.75 = f32[4,320,768]{2,1,0:T(8,128)} convert(bf16[4,320,768]{2,1,0:T(8,128)(2,1)} %reduce-scatter.4.cloned.1.call-done) | non-fusion elementwise | flops 983040 | bytes 5898240 | tf_op jit(solution)/shard_map/convert_element_type | solution.py:95
  352.2 28.3 %reduce-scatter.6.cloned.1.call-done = bf16[4,320,768]{2,1,0:T(8,128)(2,1)} async-done(((bf16[4,1280,768]{2,1,0:T(8,128)(2,1)}), bf16[4,320,768]{2,1,0:T(8,128)(2,1)}) %reduce-scatter.6.cloned.1.call-update) | async-done | bytes 1966096 | tf_op jit(solution)/shard_map/reduce_scatter | solution.py:96
  380.5 3.8 convert_element_type.77
  (66 shorter events, 36.5 us)
Async XLA Ops:
  7.2 14.1 %copy-start = (bf16[128,1280]{1,0:T(8,128)(2,1)S(1)}, bf16[128,1280]{1,0:T(8,128)(2,1)}, u32[]{:S(2)}) copy-start(bf16[128,1280]{1,0:T(8,128)(2,1)} %param.12) | copy-start | bytes 983044
  29.8 6.5 %copy-start.2 = (bf16[128,1280]{1,0:T(8,128)(2,1)S(1)}, bf16[128,1280]{1,0:T(8,128)(2,1)}, u32[]{:S(2)}) copy-start(bf16[128,1280]{1,0:T(8,128)(2,1)} %param.11) | copy-start | bytes 983044
  29.8 58.9 %all-to-all-start.2 = ((bf16[16,52,1280]{2,1,0:T(8,128)(2,1)}), bf16[16,52,1280]{2,1,0:T(8,128)(2,1)S(1)}, u32[]{:S(2)}, u32[]{:S(2)}) async-start(bf16[16,52,1280]{2,1,0:T(8,128)(2,1)} %reshape.103), calls=%async_computation.2 | async-start | bytes 4587520 | tf_op jit(solution)/shard_map/all_to_all | solution.py:80
  88.6 56.5 %all-to-all-start = ((bf16[16,52,1280]{2,1,0:T(8,128)(2,1)}), bf16[16,52,1280]{2,1,0:T(8,128)(2,1)}, u32[]{:S(2)}, u32[]{:S(2)}) async-start(bf16[16,52,1280]{2,1,0:T(8,128)(2,1)} %reshape.100), calls=%async_computation | async-start | bytes 4587520 | tf_op jit(solution)/shard_map/all_to_all | solution.py:77
  93.1 251.3 %reduce-scatter.8.cloned.1.call-start = ((), (), s32[]{:S(2)}) async-start(), calls=%async_computation.9 | async-start | bytes 9830400 | tf_op jit(solution)/shard_map/reduce_scatter | solution.py:97
  145.1 7.8 %slice-start = ((s8[7864320]{0:T(1024)(128)(4,1)}), s8[4194304]{0:T(1024)(128)(4,1)S(1)}, s32[]{:S(2)}) async-start(s8[7864320]{0:T(1024)(128)(4,1)} %bitcast.48), calls=%async_computation.10 | async-start | bytes 8388608
  147.7 5.2 %slice-start.1 = ((s8[7864320]{0:T(1024)(128)(4,1)}), s8[3670016]{0:T(1024)(128)(4,1)S(1)}, s32[]{:S(2)}) async-start(s8[7864320]{0:T(1024)(128)(4,1)} %bitcast.48), calls=%async_computation.11 | async-start | bytes 7340032
  153.0 1.8 copy-start.3
  162.5 1.0 copy-start.5
  168.9 179.3 %reduce-scatter.4.cloned.1.call-start = ((), (), s32[]{:S(2)}) async-start(), calls=%async_computation.7 | async-start | bytes 9830400 | tf_op jit(solution)/shard_map/reduce_scatter | solution.py:95
  177.1 203.4 %reduce-scatter.6.cloned.1.call-start = ((), (), s32[]{:S(2)}) async-start(), calls=%async_computation.8 | async-start | bytes 9830400 | tf_op jit(solution)/shard_map/reduce_scatter | solution.py:96
  184.4 1.3 copy-start.4
  185.7 5.9 %copy-start.6 = (bf16[4,208,768]{2,1,0:T(8,128)(2,1)S(1)}, bf16[4,208,768]{2,1,0:T(8,128)(2,1)}, u32[]{:S(2)}) copy-start(bf16[4,208,768]{2,1,0:T(8,128)(2,1)} %get-tuple-element.13) | copy-start | bytes 3833860
  200.4 52.4 %all-to-all-start.3 = ((bf16[4,208,1280]{2,0,1:T(4,128)(2,1)}), bf16[4,208,1280]{2,0,1:T(4,128)(2,1)S(1)}, u32[]{:S(2)}, u32[]{:S(2)}) async-start(bf16[4,208,1280]{2,0,1:T(4,128)(2,1)} %copy.50), calls=%async_computation.3 | async-start | bytes 4259840 | tf_op jit(solution)/shard_map/all_to_all | solution.py:84
  212.1 45.5 %copy-start.8 = (bf16[128,6]{0,1:T(8,128)(2,1)S(1)}, bf16[128,6]{0,1:T(8,128)(2,1)}, u32[]{:S(2)}) copy-start(bf16[128,6]{0,1:T(8,128)(2,1)} %param.14) | copy-start | bytes 4612
  252.8 52.9 %all-to-all-start.1 = ((bf16[4,208,1280]{2,0,1:T(4,128)(2,1)}), bf16[4,208,1280]{2,0,1:T(4,128)(2,1)}, u32[]{:S(2)}, u32[]{:S(2)}) async-start(bf16[4,208,1280]{2,0,1:T(4,128)(2,1)} %copy.44), calls=%async_computation.1 | async-start | bytes 4259840 | tf_op jit(solution)/shard_map/all_to_all | solution.py:79
  316.7 7.7 %copy-start.7 = (bf16[768,1280]{1,0:T(8,128)(2,1)S(1)}, bf16[768,1280]{1,0:T(8,128)(2,1)}, u32[]{:S(2)}) copy-start(bf16[768,1280]{1,0:T(8,128)(2,1)} %gather_fusion.4) | copy-start | bytes 5898244
  348.2 36.1 %copy-start.1 = (bf16[128,1280]{1,0:T(8,128)(2,1)S(1)}, bf16[128,1280]{1,0:T(8,128)(2,1)}, u32[]{:S(2)}) copy-start(bf16[128,1280]{1,0:T(8,128)(2,1)} %param.12) | copy-start | bytes 983044
Sparse Core Ops, SparseCore 0:
  169.1 68.0 reduce-scatter.7
  239.9 68.9 reduce-scatter.3
  311.5 68.9 reduce-scatter.5
where the time goes:
time: 392 us; the launch traced here: 391 us
  waiting for transfers between devices  204 us (52%)
  local copies, waits for them, and re-layouts  68.8 us (18%)
  matrix products  53.1 us (14%)
  other arithmetic  31.3 us (8%)
  starting transfers between devices  19.8 us (5%)
  between operations  14 us (4%)
    all_to_all x1, waiting for transfers between devices, shards(): lax.all_to_all(sent_tokens, 'expert', split_axis=0, concat_axis=1, tiled=...  49.6 us
    all_to_all x1, waiting for transfers between devices, shards(): lax.all_to_all(expert_out, 'expert', split_axis=1, concat_axis=0, tiled=T...  43.8 us
    all_to_all x1, waiting for transfers between devices, shards(): lax.all_to_all(sent_grads, 'expert', split_axis=0, concat_axis=1, tiled=T...  41.2 us
    all_to_all x1, waiting for transfers between devices, shards(): lax.all_to_all(slot_grad, 'expert', split_axis=1, concat_axis=0, tiled=True)  40.7 us
    reduce_scatter x1, waiting for transfers between devices, shards(): lax.psum_scatter(part_up, 'dp', scatter_dimension=1, tiled=True)  28.3 us
    gather x2, local copies, waits for them, and re-layouts, collect(): jnp.take(returned_rows.reshape(experts * capacity, model_width), slot_des...  11.4 us
    dot_general x1, matrix products, expert_backward(): jnp.einsum('erd,erf->edf', inputs, gate_back, preferred_element_type=jnp....  8.1 us
  transfers between devices with their start and end apart: 7, of which 5 were waited for; matrix products, arithmetic and copies ran while one was open for 26% of the time, Pallas kernels for 0%

commit v1 on v0

--- a/solution.py
+++ b/solution.py
@@ -1,6 +1,10 @@
+import functools
+
 import jax
 import jax.numpy as jnp
 from jax import lax
+from jax.experimental import pallas as pl
+from jax.experimental.pallas import tpu as pltpu
 from jax.sharding import PartitionSpec as P
 
 
@@ -99,9 +103,176 @@
     return (layer_out, grad_tokens, grad_gate, grad_up, grad_down)
 
 
+def gathered_kernel(sizes, place_ref, tok_ref, cot_ref, wg_ref, wu_ref, wd_ref, out_ref, gtok_ref, gg_ref, gu_ref, gd_ref,
+                    rank_s, gate_s, x_s, og_s, h_s, gb_s, ub_s, xs_s, hs_s, p_s, pg_s, out_acc, gtok_acc):
+    peers, reps, rows, width, ff, exp_local, queue = sizes
+    f32, bf16 = jnp.float32, jnp.bfloat16
+    group = peers * rows
+    expert = pl.program_id(0)
+    own_rep = place_ref[1]
+    expert_row = place_ref[0] * exp_local + expert
+    dot = functools.partial(lax.dot_general, preferred_element_type=f32)
+    nn, nt, tn = (((1,), (0,)), ((), ())), (((1,), (1,)), ((), ())), (((0,), (0,)), ((), ()))
+
+    @pl.when(expert == 0)
+    def _():
+        out_acc[...] = jnp.zeros_like(out_acc)
+        gtok_acc[...] = jnp.zeros_like(gtok_acc)
+        before = lax.broadcasted_iota(jnp.int32, (group, group), 0)
+        after = lax.broadcasted_iota(jnp.int32, (group, group), 1)
+        triangle = jnp.where(before < after, 1.0, 0.0).astype(bf16)
+        unit = jnp.where(before == after, 1.0, 0.0).astype(bf16)
+
+        def tables(rep, carry):
+            gates = tok_ref[:, rep, :, width:].reshape(group, tok_ref.shape[3] - width)
+            chosen = jnp.where(gates.astype(f32) > 0.0, 1.0, 0.0).astype(bf16)
+            gate_rows = dot(gates, unit, tn)
+            rank_s[rep] = jnp.where(gate_rows > 0.0, dot(chosen, triangle, tn), -1.0)
+            gate_s[rep] = gate_rows
+            return carry
+
+        lax.fori_loop(0, reps, tables, 0)
+
+    def pick(rep, carry):
+        rank = rank_s[rep, pl.ds(expert_row, 1), :]
+        gate = gate_s[rep, pl.ds(expert_row, 1), :]
+        match = lax.broadcasted_iota(jnp.int32, (queue, group), 0) == rank.astype(jnp.int32)
+        choice = jnp.where(match, 1.0, 0.0).astype(bf16)
+        gated = jnp.where(match, jnp.broadcast_to(gate, (queue, group)), 0.0).astype(bf16)
+        at = pl.multiple_of(rep * queue, queue)
+        x_s[pl.ds(at, queue), :] = dot(choice, tok_ref[:, rep, :, :width].reshape(group, width), nn).astype(bf16)
+        og_s[pl.ds(at, queue), :] = dot(gated, cot_ref[:, rep].reshape(group, width), nn).astype(bf16)
+
+        @pl.when(rep == own_rep)
+        def _():
+            p_s[...] = choice
+            pg_s[...] = gated
+
+        return carry
+
+    lax.fori_loop(0, reps, pick, 0)
+
+    tile = 256
+    half = reps * queue // 2
+
+    def middle(step, carry):
+        col = pl.ds(pl.multiple_of(step // 2 * tile, tile), tile)
+        row = pl.ds(pl.multiple_of(step % 2 * half, half), half)
+        x = x_s[row, :]
+        gate_sums = dot(x, wg_ref[0, :, col], nn)
+        up_sums = dot(x, wu_ref[0, :, col], nn)
+        hidden_grad = dot(og_s[row, :], wd_ref[0, col, :], nt)
+        sigmoid = jax.nn.sigmoid(gate_sums)
+        act = gate_sums * sigmoid
+        h_s[row, col] = (act * up_sums).astype(bf16)
+        gb_s[row, col] = (hidden_grad * up_sums * sigmoid * (1.0 + gate_sums * (1.0 - sigmoid))).astype(bf16)
+        ub_s[row, col] = (hidden_grad * act).astype(bf16)
+        return carry
+
+    lax.fori_loop(0, ff // tile * 2, middle, 0)
+
+    own = pl.ds(pl.multiple_of(own_rep * queue, queue), queue)
+
+    def returns(step, carry):
+        col = pl.ds(pl.multiple_of(step * tile, tile), tile)
+        expert_out = dot(h_s[own, :], wd_ref[0, :, col], nn).astype(bf16)
+        out_acc[:, col] += dot(pg_s[...], expert_out, tn)
+        slot_grad = (dot(gb_s[own, :], wg_ref[0, col, :], nt) + dot(ub_s[own, :], wu_ref[0, col, :], nt)).astype(bf16)
+        gtok_acc[:, col] += dot(p_s[...], slot_grad, tn)
+        return carry
+
+    lax.fori_loop(0, width // tile, returns, 0)
+
+    wide, narrow = width // reps, ff // reps
+    for rep in range(reps):
+        @pl.when(own_rep == rep)
+        def _():
+            xs_s[...] = x_s[:, rep * wide:(rep + 1) * wide]
+            hs_s[...] = h_s[:, rep * narrow:(rep + 1) * narrow]
+
+    def sums(step, carry):
+        col = pl.ds(pl.multiple_of(step * tile, tile), tile)
+        gg_ref[0, :, col] = dot(xs_s[...], gb_s[:, col], tn)
+        gu_ref[0, :, col] = dot(xs_s[...], ub_s[:, col], tn)
+        return carry
+
+    lax.fori_loop(0, ff // tile, sums, 0)
+
+    def sums_down(step, carry):
+        col = pl.ds(pl.multiple_of(step * tile, tile), tile)
+        gd_ref[0, :, col] = dot(hs_s[...], og_s[:, col], tn)
+        return carry
+
+    lax.fori_loop(0, width // tile, sums_down, 0)
+
+    @pl.when(expert == exp_local - 1)
+    def _():
+        out_ref[...] = out_acc[...].astype(bf16)
+        gtok_ref[...] = gtok_acc[...].astype(bf16)
+
+
+def gathered_shards(tokens, cotangent, expert_ids, gate_values, gate_weight, up_weight, down_weight):
+    rows, width = tokens.shape
+    top_count = expert_ids.shape[1]
+    exp_local, _, ff = gate_weight.shape
+    peers, reps = lax.axis_size("expert"), lax.axis_size("dp")
+    experts = exp_local * peers
+    slots = rows * top_count
+    queue = (slots + slots // 12) // experts * peers
+    f32, bf16 = jnp.float32, jnp.bfloat16
+    lanes = 128
+    chosen = expert_ids[:, :, None] == jnp.arange(lanes, dtype=jnp.int32)[None, None, :]
+    gates = jnp.sum(jnp.where(chosen, gate_values[:, :, None].astype(f32), 0.0), axis=1).astype(bf16)
+    packed = jnp.concatenate([tokens, gates], axis=1)
+    tok_all = lax.all_gather(packed, ("expert", "dp"), axis=0, tiled=True).reshape(peers, reps, rows, width + lanes)
+    cot_all = lax.all_gather(cotangent, ("expert", "dp"), axis=0, tiled=True).reshape(peers, reps, rows, width)
+    place = jnp.stack([lax.axis_index("expert"), lax.axis_index("dp")]).astype(jnp.int32)
+    sizes = (peers, reps, rows, width, ff, exp_local, queue)
+    group, every = peers * rows, reps * queue
+    whole = lambda shape: pl.BlockSpec(shape, lambda e, *_: (0,) * len(shape), pipeline_mode=pl.Buffered(1))
+    each = lambda a, b: pl.BlockSpec((1, a, b), lambda e, *_: (e, 0, 0))
+    out, gtok, gg, gu, gd = pl.pallas_call(
+        functools.partial(gathered_kernel, sizes),
+        grid_spec=pltpu.PrefetchScalarGridSpec(
+            num_scalar_prefetch=1,
+            grid=(exp_local,),
+            in_specs=[whole(tok_all.shape), whole(cot_all.shape), each(width, ff), each(width, ff), each(ff, width)],
+            out_specs=[whole((group, width)), whole((group, width)), each(width // reps, ff), each(width // reps, ff), each(ff // reps, width)],
+            scratch_shapes=[
+                pltpu.VMEM((reps, lanes, group), f32),
+                pltpu.VMEM((reps, lanes, group), f32),
+                pltpu.VMEM((every, width), bf16),
+                pltpu.VMEM((every, width), bf16),
+                pltpu.VMEM((every, ff), bf16),
+                pltpu.VMEM((every, ff), bf16),
+                pltpu.VMEM((every, ff), bf16),
+                pltpu.VMEM((every, width // reps), bf16),
+                pltpu.VMEM((every, ff // reps), bf16),
+                pltpu.VMEM((queue, group), bf16),
+                pltpu.VMEM((queue, group), bf16),
+                pltpu.VMEM((group, width), f32),
+                pltpu.VMEM((group, width), f32),
+            ],
+        ),
+        out_shape=[
+            jax.ShapeDtypeStruct((group, width), bf16),
+            jax.ShapeDtypeStruct((group, width), bf16),
+            jax.ShapeDtypeStruct((exp_local, width // reps, ff), f32),
+            jax.ShapeDtypeStruct((exp_local, width // reps, ff), f32),
+            jax.ShapeDtypeStruct((exp_local, ff // reps, width), f32),
+        ],
+        compiler_params=pltpu.CompilerParams(vmem_limit_bytes=60 * 1024 * 1024),
+    )(place, tok_all, cot_all, gate_weight, up_weight, down_weight)
+    layer_out = lax.psum_scatter(out, "expert", scatter_dimension=0, tiled=True)
+    grad_tokens = lax.psum_scatter(gtok, "expert", scatter_dimension=0, tiled=True)
+    return (layer_out, grad_tokens, gg, gu, gd)
+
+
 def solution(mesh):
+    blocks = mesh.shape["expert"] * mesh.shape["dp"]
+    body = gathered_shards if blocks <= 16 else shards
     return jax.shard_map(
-        shards,
+        body,
         mesh=mesh,
         in_specs=(
             P(("groups", "expert", "dp"), None),

time: 392 us -> 281 us (0.72)
  Pallas kernels: 0 us -> 80.9 us
  local copies, waits for them, and re-layouts: 68.8 us -> 0 us
  matrix products: 53.1 us -> 0 us
  other arithmetic: 31.3 us -> 4.02 us
  waiting for transfers between devices: 204 us -> 182 us
  starting transfers between devices: 19.8 us -> 0.16 us
    all_to_all x4 -> x0, waiting for transfers between devices: 175 us -> none  [the longest x1 49.6 us: shards(): lax.all_to_all(sent_tokens, 'expert', split_axis=0, concat_axis=1, tiled=...]
    all_gather x0 -> x2, waiting for transfers between devices: none -> 117 us  [the longest x1 60.5 us: gathered_shards(): lax.all_gather(packed, ('expert', 'dp'), axis=0, tiled=True)]
    pallas_call x0 -> x1, Pallas kernels: none -> 80.9 us  [gathered_shards(): pl.pallas_call(functools.partial(gathered_kernel, sizes), grid_spec=pltpu...]
    dot_general x9 -> x0, matrix products: 53.1 us -> none  [the longest x1 8.1 us: expert_backward(): jnp.einsum('erd,erf->edf', inputs, gate_back, preferred_element_type=jnp....]
    reduce_scatter x3 -> x2, waiting for transfers between devices: 28.3 us -> 63.4 us  [the longest x1 32.8 us: gathered_shards(): lax.psum_scatter(gtok, 'expert', scatter_dimension=0, tiled=True)]
    gather x5 -> x0, local copies, waits for them, and re-layouts: 25.4 us -> none  [the longest x2 11.4 us: collect(): jnp.take(returned_rows.reshape(experts * capacity, model_width), slot_des...]
    all_to_all x4 -> x0, starting transfers between devices: 19.3 us -> none  [the longest x1 6.45 us: shards(): lax.all_to_all(sent_grads, 'expert', split_axis=0, concat_axis=1, tiled=T...]
    reshape x6 -> x0, local copies, waits for them, and re-layouts: 15.6 us -> none  [the longest x2 6.5 us: collect(): returned_rows.reshape(experts * capacity, model_width)]
  transfers between devices with their start and end apart: 7 -> 4, of which waited for: 5 -> 4; matrix products, arithmetic and copies ran while one was open for 26% -> 1% of each run, Pallas kernels for 0% -> 0%
where the time goes in v1:
time: 281 us
  waiting for transfers between devices  182 us (65%)
  Pallas kernels  80.9 us (29%)
  between operations  13.8 us (5%)
  other arithmetic  4.02 us (1%)
    pallas_call x1, Pallas kernels, gathered_shards(): pl.pallas_call(functools.partial(gathered_kernel, sizes), grid_spec=pltpu...  80.9 us
    all_gather x1, waiting for transfers between devices, gathered_shards(): lax.all_gather(packed, ('expert', 'dp'), axis=0, tiled=True)  60.5 us
    all_gather x1, waiting for transfers between devices, gathered_shards(): lax.all_gather(cotangent, ('expert', 'dp'), axis=0, tiled=True)  56.9 us
    reduce_scatter x1, waiting for transfers between devices, gathered_shards(): lax.psum_scatter(gtok, 'expert', scatter_dimension=0, tiled=True)  32.8 us
    reduce_scatter x1, waiting for transfers between devices, gathered_shards(): layer_out = lax.psum_scatter(out, 'expert', scatter_dimension=0, tiled=True)  30.6 us
  transfers between devices with their start and end apart: 4, of which 4 were waited for; matrix products, arithmetic and copies ran while one was open for 1% of the time, Pallas kernels for 0%

profile of v1, /device:TPU:0, one launch (start us, length us, event | category | flops | bytes accessed | tf_op | source)
XLA Modules:
  0.0 280.9 jit_solution(14836899135972738059)
XLA Ops:
  7.2 0.0 all-gather.5.cloned.1.call-start
  7.2 0.7 all-gather.5.cloned.1.call-update
  7.9 0.0 all-gather.3.cloned.1.call-start
  7.9 0.7 convert_element_type.7
  8.6 1.0 select_reduce_fusion
  9.6 1.7 pad_maximum_fusion
  11.3 0.0 all-gather.3.cloned.1.call-update
  11.3 0.0 reduce-scatter.3.cloned.1.call-start
  11.4 0.7 pad_add_fusion.place_ref
  12.1 56.9 %all-gather.5.cloned.1.call-done = bf16[2048,1280]{1,0:T(8,128)(2,1)} async-done(((bf16[128,1280]{1,0:T(8,128)(2,1)}), bf16[2048,1280]{1,0:T(8,128)(2,1)}) %all-gather.5.cloned.1.call-update) | async-done | bytes 5242896 | tf_op jit(solution)/shard_map/all_gather | solution.py:228
  69.0 60.5 %all-gather.3.cloned.1.call-done = bf16[2048,1408]{1,0:T(8,128)(2,1)} async-done(((bf16[128,1408]{1,0:T(8,128)(2,1)}), bf16[2048,1408]{1,0:T(8,128)(2,1)}) %all-gather.3.cloned.1.call-update) | async-done | bytes 5767184 | tf_op jit(solution)/shard_map/all_gather | solution.py:227
  129.5 80.9 %shard_map.110 = (bf16[512,1280]{1,0:T(8,128)(2,1)}, bf16[512,1280]{1,0:T(8,128)(2,1)}, f32[4,320,768]{2,1,0:T(8,128)}, f32[4,320,768]{2,1,0:T(8,128)}, f32[4,192,1280]{2,1,0:T(8,128)}) custom-call(s32[2]{0:T(128)} %pad_add_fusion.place_ref, bf16[4,4,128,1408]{3,2,1,0:T(8,128)(2,1)} %bitcast.4, bf16[4,4,128,1280]{3,2,1,0:T(8,128)(2,1)} %bitcast.5, ...), custom_call_target="tpu_custom_call" | custom-call | tf_op jit(solution)/shard_map/pallas_call | solution.py:234
  210.3 0.0 reduce-scatter.3.cloned.1.call-update
  210.4 0.0 reduce-scatter.5.cloned.1.call-start
  210.4 0.5 reduce-scatter.5.cloned.1.call-update
  211.0 30.6 %reduce-scatter.3.cloned.1.call-done = bf16[128,1280]{1,0:T(8,128)(2,1)} async-done(((bf16[512,1280]{1,0:T(8,128)(2,1)}), bf16[128,1280]{1,0:T(8,128)(2,1)}) %reduce-scatter.3.cloned.1.call-update) | async-done | bytes 327696 | tf_op jit(solution)/shard_map/reduce_scatter | solution.py:266
  241.5 32.8 %reduce-scatter.5.cloned.1.call-done = bf16[128,1280]{1,0:T(8,128)(2,1)} async-done(((bf16[512,1280]{1,0:T(8,128)(2,1)}), bf16[128,1280]{1,0:T(8,128)(2,1)}) %reduce-scatter.5.cloned.1.call-update) | async-done | bytes 327696 | tf_op jit(solution)/shard_map/reduce_scatter | solution.py:267
Async XLA Ops:
  7.2 61.8 %all-gather.5.cloned.1.call-start = ((), (), s32[]{:S(2)}) async-start(), calls=%async_computation.3 | async-start | bytes 5570560 | tf_op jit(solution)/shard_map/all_gather | solution.py:228
  7.9 121.6 %all-gather.3.cloned.1.call-start = ((), (), s32[]{:S(2)}) async-start(), calls=%async_computation.2 | async-start | bytes 6127616 | tf_op jit(solution)/shard_map/all_gather | solution.py:227
  11.3 230.2 %reduce-scatter.3.cloned.1.call-start = ((), (), s32[]{:S(2)}) async-start(), calls=%async_computation.4 | async-start | bytes 1638400 | tf_op jit(solution)/shard_map/reduce_scatter | solution.py:266
  210.4 64.0 %reduce-scatter.5.cloned.1.call-start = ((), (), s32[]{:S(2)}) async-start(), calls=%async_computation.5 | async-start | bytes 1638400 | tf_op jit(solution)/shard_map/reduce_scatter | solution.py:267
Sparse Core Ops, SparseCore 0:
  10.3 58.6 all-gather.4
  71.9 57.5 all-gather.2
  210.5 31.0 reduce-scatter.2
  244.3 30.0 reduce-scatter.4

commit v2 on v0

--- a/solution.py
+++ b/solution.py
@@ -1,6 +1,10 @@
+import functools
+
 import jax
 import jax.numpy as jnp
 from jax import lax
+from jax.experimental import pallas as pl
+from jax.experimental.pallas import tpu as pltpu
 from jax.sharding import PartitionSpec as P
 
 
@@ -99,9 +103,283 @@
     return (layer_out, grad_tokens, grad_gate, grad_up, grad_down)
 
 
+MESH = pl.DeviceIdType.MESH
+
+
+def fused_kernel(sizes, tok_ref, cot_ref, wg_ref, wu_ref, wd_ref, out_ref, gtok_ref, gg_ref, gu_ref, gd_ref,
+                 tok_s, cot_s, rank_s, gate_s, x_s, og_s, h_s, gb_s, ub_s, xs_s, hs_s, p_s, pg_s, out_acc, gtok_acc,
+                 stage_s, land_s, send_sem, recv_sem, back_send, back_recv):
+    peers, reps, rows, width, ff, exp_local, queue = sizes
+    f32, bf16 = jnp.float32, jnp.bfloat16
+    group = peers * rows
+    phase, expert = pl.program_id(0), pl.program_id(1)
+    me, rep_me = lax.axis_index("expert"), lax.axis_index("dp")
+    core, side = rep_me % 2, rep_me // 2
+    mate = side * 2 + (1 - core)
+    across = (1 - side) * 2 + core
+    across_mate = (1 - side) * 2 + (1 - core)
+    expert_row = me * exp_local + expert
+    dot = functools.partial(lax.dot_general, preferred_element_type=f32)
+    nn, nt, tn = (((1,), (0,)), ((), ())), (((1,), (1,)), ((), ())), (((0,), (0,)), ((), ()))
+    kept = (tok_s, cot_s)
+
+    def push(what, where, rep, place, device, source=None):
+        block = kept[what].at[where, rep]
+        return pltpu.make_async_remote_copy(
+            src_ref=block if source is None else source,
+            dst_ref=block,
+            send_sem=send_sem.at[what, place],
+            recv_sem=recv_sem.at[what, where, rep],
+            device_id=device,
+            device_id_type=MESH,
+        )
+
+    def spread(what, where, offset, source=None):
+        push(what, where, rep_me, peers - 1 + offset, {"dp": across}, source).start()
+        push(what, where, rep_me, 2 * peers - 1 + offset, {"dp": mate}, source).start()
+
+    def arrive(what, where, rep):
+        push(what, where, rep, 0, {"dp": mate}).wait_recv()
+
+    def back(which, offset):
+        return pltpu.make_async_remote_copy(
+            src_ref=stage_s.at[which, lax.rem(me + offset, peers)],
+            dst_ref=land_s.at[which, me],
+            send_sem=back_send.at[which, offset - 1],
+            recv_sem=back_recv.at[which, me],
+            device_id={"expert": lax.rem(me + offset, peers)},
+            device_id_type=MESH,
+        )
+
+    @pl.when((phase == 0) & (expert == 0))
+    def _():
+        barrier = pltpu.get_barrier_semaphore()
+        for offset in range(1, peers):
+            pl.semaphore_signal(barrier, inc=1, device_id={"expert": lax.rem(me + offset, peers)}, device_id_type=MESH)
+        for rep in (mate, across):
+            pl.semaphore_signal(barrier, inc=1, device_id={"dp": rep}, device_id_type=MESH)
+        pl.semaphore_wait(barrier, peers + 1)
+        own = (tok_ref, cot_ref)
+        for what in range(2):
+            for offset in range(1, peers):
+                push(what, me, rep_me, offset - 1, {"expert": lax.rem(me + offset, peers)}, own[what]).start()
+            spread(what, me, 0, own[what])
+        tok_s[me, rep_me] = tok_ref[...]
+        cot_s[me, rep_me] = cot_ref[...]
+        out_acc[...] = jnp.zeros_like(out_acc)
+        gtok_acc[...] = jnp.zeros_like(gtok_acc)
+        for what in range(2):
+            for offset in range(1, peers):
+                where = lax.rem(me + peers - offset, peers)
+                arrive(what, where, rep_me)
+                spread(what, where, offset)
+        for what in range(2):
+            for offset in range(peers):
+                arrive(what, lax.rem(me + peers - offset, peers), mate)
+
+    @pl.when((phase == 0) & (expert == 1))
+    def _():
+        for what in range(2):
+            for offset in range(peers):
+                where = lax.rem(me + peers - offset, peers)
+                arrive(what, where, across)
+                push(what, where, across, 3 * peers - 1 + offset, {"dp": mate}).start()
+
+    @pl.when((phase == 1) & (expert == 0))
+    def _():
+        for what in range(2):
+            for offset in range(peers):
+                arrive(what, lax.rem(me + peers - offset, peers), across_mate)
+
+    first = (side + phase) % 2 * 2
+
+    @pl.when(expert == 0)
+    def _():
+        before = lax.broadcasted_iota(jnp.int32, (group, group), 0)
+        after = lax.broadcasted_iota(jnp.int32, (group, group), 1)
+        triangle = jnp.where(before < after, 1.0, 0.0).astype(bf16)
+        unit = jnp.where(before == after, 1.0, 0.0).astype(bf16)
+
+        def tables(at, carry):
+            gates = tok_s[:, first + at, :, width:].reshape(group, tok_s.shape[3] - width)
+            chosen = jnp.where(gates.astype(f32) > 0.0, 1.0, 0.0).astype(bf16)
+            gate_rows = dot(gates, unit, tn)
+            rank_s[at] = jnp.where(gate_rows > 0.0, dot(chosen, triangle, tn), -1.0)
+            gate_s[at] = gate_rows
+            return carry
+
+        lax.fori_loop(0, 2, tables, 0)
+
+    def pick(at, carry):
+        rank = rank_s[at, pl.ds(expert_row, 1), :]
+        gate = gate_s[at, pl.ds(expert_row, 1), :]
+        match = lax.broadcasted_iota(jnp.int32, (queue, group), 0).astype(f32) == rank
+        choice = jnp.where(match, 1.0, 0.0).astype(bf16)
+        gated = jnp.where(match, jnp.broadcast_to(gate, (queue, group)), 0.0).astype(bf16)
+        row = pl.ds(pl.multiple_of(at * queue, queue), queue)
+        x_s[row, :] = dot(choice, tok_s[:, first + at, :, :width].reshape(group, width), nn).astype(bf16)
+        og_s[row, :] = dot(gated, cot_s[:, first + at].reshape(group, width), nn).astype(bf16)
+
+        @pl.when(at == core)
+        def _():
+            p_s[...] = choice
+            pg_s[...] = gated
+
+        return carry
+
+    lax.fori_loop(0, 2, pick, 0)
+
+    tile = 256
+
+    def middle(step, carry):
+        col = pl.ds(pl.multiple_of(step * tile, tile), tile)
+        x = x_s[...]
+        gate_sums = dot(x, wg_ref[0, :, col], nn)
+        up_sums = dot(x, wu_ref[0, :, col], nn)
+        hidden_grad = dot(og_s[...], wd_ref[0, col, :], nt)
+        sigmoid = jax.nn.sigmoid(gate_sums)
+        act = gate_sums * sigmoid
+        h_s[:, col] = (act * up_sums).astype(bf16)
+        gb_s[:, col] = (hidden_grad * up_sums * sigmoid * (1.0 + gate_sums * (1.0 - sigmoid))).astype(bf16)
+        ub_s[:, col] = (hidden_grad * act).astype(bf16)
+        return carry
+
+    lax.fori_loop(0, ff // tile, middle, 0)
+
+    @pl.when(phase == 0)
+    def _():
+        own = pl.ds(pl.multiple_of(core * queue, queue), queue)
+
+        def returns(step, carry):
+            col = pl.ds(pl.multiple_of(step * tile, tile), tile)
+            expert_out = dot(h_s[own, :], wd_ref[0, :, col], nn).astype(bf16)
+            out_acc[:, col] += dot(pg_s[...], expert_out, tn)
+            slot_grad = (dot(gb_s[own, :], wg_ref[0, col, :], nt) + dot(ub_s[own, :], wu_ref[0, col, :], nt)).astype(bf16)
+            gtok_acc[:, col] += dot(p_s[...], slot_grad, tn)
+            return carry
+
+        lax.fori_loop(0, width // tile, returns, 0)
+
+    @pl.when((phase == 0) & (expert == exp_local - 1))
+    def _():
+        for which, acc in enumerate((out_acc, gtok_acc)):
+            stage_s[which] = acc[...].astype(bf16).reshape(peers, rows, width)
+            for offset in range(1, peers):
+                back(which, offset).start()
+
+    wide, narrow = width // reps, ff // reps
+    for rep in range(reps):
+        @pl.when(rep_me == rep)
+        def _():
+            xs_s[...] = x_s[:, rep * wide:(rep + 1) * wide]
+            hs_s[...] = h_s[:, rep * narrow:(rep + 1) * narrow]
+
+    @pl.when(phase == 0)
+    def _():
+        gg_ref[expert] = jnp.zeros((wide, ff), f32)
+        gu_ref[expert] = jnp.zeros((wide, ff), f32)
+        gd_ref[expert] = jnp.zeros((narrow, width), f32)
+
+    def sums(step, carry):
+        col = pl.ds(pl.multiple_of(step * tile, tile), tile)
+        gg_ref[expert, :, col] += dot(xs_s[...], gb_s[:, col], tn)
+        gu_ref[expert, :, col] += dot(xs_s[...], ub_s[:, col], tn)
+        return carry
+
+    lax.fori_loop(0, ff // tile, sums, 0)
+
+    def sums_down(step, carry):
+        col = pl.ds(pl.multiple_of(step * tile, tile), tile)
+        gd_ref[expert, :, col] += dot(hs_s[...], og_s[:, col], tn)
+        return carry
+
+    lax.fori_loop(0, width // tile, sums_down, 0)
+
+    @pl.when((phase == 1) & (expert == exp_local - 1))
+    def _():
+        for which, (acc, ref) in enumerate(((out_acc, out_ref), (gtok_acc, gtok_ref))):
+            total = acc[pl.ds(pl.multiple_of(me * rows, rows), rows), :]
+            for offset in range(1, peers):
+                where = lax.rem(me + peers - offset, peers)
+                pltpu.make_async_remote_copy(
+                    src_ref=stage_s.at[which, 0],
+                    dst_ref=land_s.at[which, where],
+                    send_sem=back_send.at[which, 0],
+                    recv_sem=back_recv.at[which, where],
+                    device_id={"dp": mate},
+                    device_id_type=MESH,
+                ).wait_recv()
+                total = total + land_s[which, where].astype(f32)
+            ref[...] = total.astype(bf16)
+        for which in range(2):
+            for offset in range(1, peers):
+                back(which, offset).wait_send()
+            for place in range(4 * peers - 1):
+                push(which, me, rep_me, place, {"dp": mate}).wait_send()
+
+
+def fused_shards(tokens, cotangent, expert_ids, gate_values, gate_weight, up_weight, down_weight):
+    rows, width = tokens.shape
+    top_count = expert_ids.shape[1]
+    exp_local, _, ff = gate_weight.shape
+    peers, reps = lax.axis_size("expert"), lax.axis_size("dp")
+    experts = exp_local * peers
+    slots = rows * top_count
+    queue = (slots + slots // 12) // experts * peers
+    f32, bf16 = jnp.float32, jnp.bfloat16
+    lanes = 128
+    chosen = expert_ids[:, :, None] == jnp.arange(lanes, dtype=jnp.int32)[None, None, :]
+    gates = jnp.sum(jnp.where(chosen, gate_values[:, :, None].astype(f32), 0.0), axis=1).astype(bf16)
+    packed = jnp.concatenate([tokens, gates], axis=1)
+    sizes = (peers, reps, rows, width, ff, exp_local, queue)
+    group, every = peers * rows, 2 * queue
+    wide, narrow = width // reps, ff // reps
+    whole = lambda *shape: pl.BlockSpec(shape, lambda p, e: (0,) * len(shape), pipeline_mode=pl.Buffered(1))
+    each = lambda a, b: pl.BlockSpec((1, a, b), lambda p, e: (e, 0, 0))
+    return pl.pallas_call(
+        functools.partial(fused_kernel, sizes),
+        grid=(2, exp_local),
+        in_specs=[whole(rows, width + lanes), whole(rows, width), each(width, ff), each(width, ff), each(ff, width)],
+        out_specs=[whole(rows, width), whole(rows, width), whole(exp_local, wide, ff), whole(exp_local, wide, ff), whole(exp_local, narrow, width)],
+        scratch_shapes=[
+            pltpu.VMEM((peers, reps, rows, width + lanes), bf16),
+            pltpu.VMEM((peers, reps, rows, width), bf16),
+            pltpu.VMEM((2, lanes, group), f32),
+            pltpu.VMEM((2, lanes, group), f32),
+            pltpu.VMEM((every, width), bf16),
+            pltpu.VMEM((every, width), bf16),
+            pltpu.VMEM((every, ff), bf16),
+            pltpu.VMEM((every, ff), bf16),
+            pltpu.VMEM((every, ff), bf16),
+            pltpu.VMEM((every, wide), bf16),
+            pltpu.VMEM((every, narrow), bf16),
+            pltpu.VMEM((queue, group), bf16),
+            pltpu.VMEM((queue, group), bf16),
+            pltpu.VMEM((group, width), f32),
+            pltpu.VMEM((group, width), f32),
+            pltpu.VMEM((2, peers, rows, width), bf16),
+            pltpu.VMEM((2, peers, rows, width), bf16),
+            pltpu.SemaphoreType.DMA((2, 4 * peers - 1)),
+            pltpu.SemaphoreType.DMA((2, peers, reps)),
+            pltpu.SemaphoreType.DMA((2, peers - 1)),
+            pltpu.SemaphoreType.DMA((2, peers)),
+        ],
+        out_shape=[
+            jax.ShapeDtypeStruct((rows, width), bf16),
+            jax.ShapeDtypeStruct((rows, width), bf16),
+            jax.ShapeDtypeStruct((exp_local, wide, ff), f32),
+            jax.ShapeDtypeStruct((exp_local, wide, ff), f32),
+            jax.ShapeDtypeStruct((exp_local, narrow, width), f32),
+        ],
+        compiler_params=pltpu.CompilerParams(vmem_limit_bytes=60 * 1024 * 1024, collective_id=0, has_side_effects=True),
+    )(packed, cotangent, gate_weight, up_weight, down_weight)
+
+
 def solution(mesh):
+    fits = mesh.shape["expert"] <= 4 and mesh.shape["dp"] == 4
+    body = fused_shards if fits else shards
     return jax.shard_map(
-        shards,
+        body,
         mesh=mesh,
         in_specs=(
             P(("groups", "expert", "dp"), None),

time: 392 us -> 195 us (0.50)
  waiting for transfers between devices: 204 us -> 0 us
  Pallas kernels: 0 us -> 174 us
  local copies, waits for them, and re-layouts: 68.8 us -> 13.4 us
  matrix products: 53.1 us -> 0 us
  other arithmetic: 31.3 us -> 3.37 us
  starting transfers between devices: 19.8 us -> 0 us
  between operations: 14 us -> 0.65 us
    all_to_all x4 -> x0, waiting for transfers between devices: 175 us -> none  [the longest x1 49.6 us: shards(): lax.all_to_all(sent_tokens, 'expert', split_axis=0, concat_axis=1, tiled=...]
    pallas_call x0 -> x1, Pallas kernels: none -> 174 us  [fused_shards(): pl.pallas_call(functools.partial(fused_kernel, sizes), grid=(2, exp_local...]
    dot_general x9 -> x0, matrix products: 53.1 us -> none  [the longest x1 8.1 us: expert_backward(): jnp.einsum('erd,erf->edf', inputs, gate_back, preferred_element_type=jnp....]
    reduce_scatter x3 -> x0, waiting for transfers between devices: 28.3 us -> none  [the longest x1 28.3 us: shards(): lax.psum_scatter(part_up, 'dp', scatter_dimension=1, tiled=True)]
    gather x5 -> x0, local copies, waits for them, and re-layouts: 25.4 us -> none  [the longest x2 11.4 us: collect(): jnp.take(returned_rows.reshape(experts * capacity, model_width), slot_des...]
    all_to_all x4 -> x0, starting transfers between devices: 19.3 us -> none  [the longest x1 6.45 us: shards(): lax.all_to_all(sent_grads, 'expert', split_axis=0, concat_axis=1, tiled=T...]
    reshape x6 -> x0, local copies, waits for them, and re-layouts: 15.6 us -> none  [the longest x2 6.5 us: collect(): returned_rows.reshape(experts * capacity, model_width)]
    convert_element_type x5 -> x1, other arithmetic: 13.7 us -> 0.68 us  [fused_shards(): gate_values[:, :, None].astype(f32)]
  transfers between devices with their start and end apart: 7 -> 0, of which waited for: 5 -> 0; matrix products, arithmetic and copies ran while one was open for 26% -> 0% of each run, Pallas kernels for 0% -> 0%
where the time goes in v2:
time: 195 us; the launch traced here: 192 us
  Pallas kernels  174 us (89%)
  local copies, waits for them, and re-layouts  13.4 us (7%)
  other arithmetic  3.37 us (2%)
    pallas_call x1, Pallas kernels, fused_shards(): pl.pallas_call(functools.partial(fused_kernel, sizes), grid=(2, exp_local...  174 us
    unnamed x9, local copies, waits for them, and re-layouts  13.4 us

profile of v2, /device:TPU:0, one launch (start us, length us, event | category | flops | bytes accessed | tf_op | source)
XLA Modules:
  0.0 191.8 jit_solution(3036617657088720520)
XLA Ops:
  0.6 0.7 convert_element_type.7
  1.3 1.0 select_reduce_fusion
  2.3 1.7 pad_maximum_fusion.tok_ref
  4.0 174.3 %shard_map.110 = (bf16[128,1280]{1,0:T(8,128)(2,1)}, bf16[128,1280]{1,0:T(8,128)(2,1)}, f32[4,320,768]{2,1,0:T(8,128)}, f32[4,320,768]{2,1,0:T(8,128)}, f32[4,192,1280]{2,1,0:T(8,128)}) custom-call(bf16[128,1408]{1,0:T(8,128)(2,1)} %pad_maximum_fusion.tok_ref, bf16[128,1280]{1,0:T(8,128)(2,1)} %cot_ref.1, bf16[4,1280,768]{2,1,0:T(8,128)(2,1)} %wg_ref.1, ...), custom_call_target="tpu_custom_call" | custom-call | tf_op jit(solution)/shard_map/pallas_call | solution.py:339
  178.3 1.7 copy.19
  180.0 1.7 copy.20
  181.7 0.0 copy-start.1
  181.7 4.6 %copy.21 = f32[4,320,768]{2,1,0:T(8,128)} copy(f32[4,320,768]{2,1,0:T(8,128)} %get-tuple-element.12) | data formatting | bytes 7864320
  186.3 0.0 copy-done.1
  186.3 0.0 copy-start
  186.3 2.0 %copy.22 = f32[4,320,768]{2,1,0:T(8,128)} copy(f32[4,320,768]{2,1,0:T(8,128)S(1)} %copy-done.1) | data formatting | bytes 7864320
  188.3 1.5 copy-done
  189.8 1.9 %copy.23 = f32[4,192,1280]{2,1,0:T(8,128)} copy(f32[4,192,1280]{2,1,0:T(8,128)S(1)} %copy-done) | data formatting | bytes 7864320
Async XLA Ops:
  181.7 4.6 %copy-start.1 = (f32[4,320,768]{2,1,0:T(8,128)S(1)}, f32[4,320,768]{2,1,0:T(8,128)}, u32[]{:S(2)}) copy-start(f32[4,320,768]{2,1,0:T(8,128)} %get-tuple-element.13) | copy-start | bytes 11796484
  186.3 3.5 %copy-start = (f32[4,192,1280]{2,1,0:T(8,128)S(1)}, f32[4,192,1280]{2,1,0:T(8,128)}, u32[]{:S(2)}) copy-start(f32[4,192,1280]{2,1,0:T(8,128)} %get-tuple-element.14) | copy-start | bytes 11796484

commit v3 on v2

--- a/solution.py
+++ b/solution.py
@@ -134,9 +134,13 @@
             device_id_type=MESH,
         )
 
-    def spread(what, where, offset, source=None):
-        push(what, where, rep_me, peers - 1 + offset, {"dp": across}, source).start()
-        push(what, where, rep_me, 2 * peers - 1 + offset, {"dp": mate}, source).start()
+    def spread(what, where, source=None):
+        push(what, where, rep_me, 2 * peers - 2 + where, {"dp": across}, source).start()
+        push(what, where, rep_me, 3 * peers - 2 + where, {"dp": mate}, source).start()
+
+    def along(what, where, distance, step, source=None):
+        place = distance if step > 0 else peers - 1 + distance
+        return push(what, where, rep_me, place, {"expert": me + step}, source)
 
     def arrive(what, where, rep):
         push(what, where, rep, 0, {"dp": mate}).wait_recv()
@@ -161,94 +165,141 @@
         pl.semaphore_wait(barrier, peers + 1)
         own = (tok_ref, cot_ref)
         for what in range(2):
-            for offset in range(1, peers):
-                push(what, me, rep_me, offset - 1, {"expert": lax.rem(me + offset, peers)}, own[what]).start()
-            spread(what, me, 0, own[what])
+            @pl.when(me < peers - 1)
+            def _():
+                along(what, me, 0, 1, own[what]).start()
+
+            @pl.when(me > 0)
+            def _():
+                along(what, me, 0, -1, own[what]).start()
+
+            spread(what, me, own[what])
         tok_s[me, rep_me] = tok_ref[...]
         cot_s[me, rep_me] = cot_ref[...]
         out_acc[...] = jnp.zeros_like(out_acc)
         gtok_acc[...] = jnp.zeros_like(gtok_acc)
+        for distance in range(1, peers):
+            for what in range(2):
+                @pl.when(me >= distance)
+                def _():
+                    arrive(what, me - distance, rep_me)
+
+                    @pl.when(me < peers - 1)
+                    def _():
+                        along(what, me - distance, distance, 1).start()
+
+                    spread(what, me - distance)
+
+                @pl.when(me + distance < peers)
+                def _():
+                    arrive(what, me + distance, rep_me)
+
+                    @pl.when(me > 0)
+                    def _():
+                        along(what, me + distance, distance, -1).start()
+
+                    spread(what, me + distance)
+
+    def relay(what):
+        for where in range(peers):
+            arrive(what, where, across)
+            push(what, where, across, 4 * peers - 2 + where, {"dp": mate}).start()
+
+    @pl.when((phase == 0) & (expert == exp_local // 2))
+    def _():
+        relay(0)
+
+    @pl.when((phase == 1) & (expert == 0))
+    def _():
         for what in range(2):
-            for offset in range(1, peers):
-                where = lax.rem(me + peers - offset, peers)
-                arrive(what, where, rep_me)
-                spread(what, where, offset)
-        for what in range(2):
-            for offset in range(peers):
-                arrive(what, lax.rem(me + peers - offset, peers), mate)
-
-    @pl.when((phase == 0) & (expert == 1))
-    def _():
-        for what in range(2):
-            for offset in range(peers):
-                where = lax.rem(me + peers - offset, peers)
-                arrive(what, where, across)
-                push(what, where, across, 3 * peers - 1 + offset, {"dp": mate}).start()
-
-    @pl.when((phase == 1) & (expert == 0))
-    def _():
-        for what in range(2):
-            for offset in range(peers):
-                arrive(what, lax.rem(me + peers - offset, peers), across_mate)
-
-    first = (side + phase) % 2 * 2
-
-    @pl.when(expert == 0)
-    def _():
-        before = lax.broadcasted_iota(jnp.int32, (group, group), 0)
-        after = lax.broadcasted_iota(jnp.int32, (group, group), 1)
-        triangle = jnp.where(before < after, 1.0, 0.0).astype(bf16)
-        unit = jnp.where(before == after, 1.0, 0.0).astype(bf16)
-
-        def tables(at, carry):
-            gates = tok_s[:, first + at, :, width:].reshape(group, tok_s.shape[3] - width)
-            chosen = jnp.where(gates.astype(f32) > 0.0, 1.0, 0.0).astype(bf16)
-            gate_rows = dot(gates, unit, tn)
-            rank_s[at] = jnp.where(gate_rows > 0.0, dot(chosen, triangle, tn), -1.0)
-            gate_s[at] = gate_rows
-            return carry
-
-        lax.fori_loop(0, 2, tables, 0)
-
-    def pick(at, carry):
-        rank = rank_s[at, pl.ds(expert_row, 1), :]
-        gate = gate_s[at, pl.ds(expert_row, 1), :]
-        match = lax.broadcasted_iota(jnp.int32, (queue, group), 0).astype(f32) == rank
-        choice = jnp.where(match, 1.0, 0.0).astype(bf16)
-        gated = jnp.where(match, jnp.broadcast_to(gate, (queue, group)), 0.0).astype(bf16)
-        row = pl.ds(pl.multiple_of(at * queue, queue), queue)
-        x_s[row, :] = dot(choice, tok_s[:, first + at, :, :width].reshape(group, width), nn).astype(bf16)
-        og_s[row, :] = dot(gated, cot_s[:, first + at].reshape(group, width), nn).astype(bf16)
-
-        @pl.when(at == core)
+            for where in range(peers):
+                arrive(what, where, mate)
+                arrive(what, where, across_mate)
+
+    tile = 256
+    wide, narrow = width // reps, ff // reps
+
+    def work(count, shift):
+        all_rows = pl.ds(0, count * queue)
+
+        @pl.when(expert == 0)
         def _():
+            before = lax.broadcasted_iota(jnp.int32, (group, group), 0)
+            after = lax.broadcasted_iota(jnp.int32, (group, group), 1)
+            triangle = jnp.where(before < after, 1.0, 0.0).astype(bf16)
+            unit = jnp.where(before == after, 1.0, 0.0).astype(bf16)
+
+            def tables(at, carry):
+                gates = tok_s[:, lax.rem(rep_me + shift + at, reps), :, width:].reshape(group, tok_s.shape[3] - width)
+                chosen = jnp.where(gates.astype(f32) > 0.0, 1.0, 0.0).astype(bf16)
+                gate_rows = dot(gates, unit, tn)
+                rank_s[at] = jnp.where(gate_rows > 0.0, dot(chosen, triangle, tn), -1.0)
+                gate_s[at] = gate_rows
+                return carry
+
+            lax.fori_loop(0, count, tables, 0)
+
+        def pick(at, carry):
+            rep = lax.rem(rep_me + shift + at, reps)
+            rank = rank_s[at, pl.ds(expert_row, 1), :]
+            gate = gate_s[at, pl.ds(expert_row, 1), :]
+            match = lax.broadcasted_iota(jnp.int32, (queue, group), 0).astype(f32) == rank
+            choice = jnp.where(match, 1.0, 0.0).astype(bf16)
+            gated = jnp.where(match, jnp.broadcast_to(gate, (queue, group)), 0.0).astype(bf16)
+            row = pl.ds(pl.multiple_of(at * queue, queue), queue)
+            x_s[row, :] = dot(choice, tok_s[:, rep, :, :width].reshape(group, width), nn).astype(bf16)
+            og_s[row, :] = dot(gated, cot_s[:, rep].reshape(group, width), nn).astype(bf16)
             p_s[...] = choice
             pg_s[...] = gated
-
-        return carry
-
-    lax.fori_loop(0, 2, pick, 0)
-
-    tile = 256
-
-    def middle(step, carry):
-        col = pl.ds(pl.multiple_of(step * tile, tile), tile)
-        x = x_s[...]
-        gate_sums = dot(x, wg_ref[0, :, col], nn)
-        up_sums = dot(x, wu_ref[0, :, col], nn)
-        hidden_grad = dot(og_s[...], wd_ref[0, col, :], nt)
-        sigmoid = jax.nn.sigmoid(gate_sums)
-        act = gate_sums * sigmoid
-        h_s[:, col] = (act * up_sums).astype(bf16)
-        gb_s[:, col] = (hidden_grad * up_sums * sigmoid * (1.0 + gate_sums * (1.0 - sigmoid))).astype(bf16)
-        ub_s[:, col] = (hidden_grad * act).astype(bf16)
-        return carry
-
-    lax.fori_loop(0, ff // tile, middle, 0)
+            return carry
+
+        lax.fori_loop(0, count, pick, 0)
+
+        def middle(step, carry):
+            col = pl.ds(pl.multiple_of(step * tile, tile), tile)
+            x = x_s[all_rows, :]
+            gate_sums = dot(x, wg_ref[0, :, col], nn)
+            up_sums = dot(x, wu_ref[0, :, col], nn)
+            hidden_grad = dot(og_s[all_rows, :], wd_ref[0, col, :], nt)
+            sigmoid = jax.nn.sigmoid(gate_sums)
+            act = gate_sums * sigmoid
+            h_s[all_rows, col] = (act * up_sums).astype(bf16)
+            gb_s[all_rows, col] = (hidden_grad * up_sums * sigmoid * (1.0 + gate_sums * (1.0 - sigmoid))).astype(bf16)
+            ub_s[all_rows, col] = (hidden_grad * act).astype(bf16)
+            return carry
+
+        lax.fori_loop(0, ff // tile, middle, 0)
+
+    def total(count, fresh):
+        all_rows = pl.ds(0, count * queue)
+        for rep in range(reps):
+            @pl.when(rep_me == rep)
+            def _():
+                xs_s[all_rows, :] = x_s[all_rows, rep * wide:(rep + 1) * wide]
+                hs_s[all_rows, :] = h_s[all_rows, rep * narrow:(rep + 1) * narrow]
+
+        def put(ref, col, value):
+            ref[expert, :, col] = value if fresh else ref[expert, :, col] + value
+
+        def sums(step, carry):
+            col = pl.ds(pl.multiple_of(step * tile, tile), tile)
+            put(gg_ref, col, dot(xs_s[all_rows, :], gb_s[all_rows, col], tn))
+            put(gu_ref, col, dot(xs_s[all_rows, :], ub_s[all_rows, col], tn))
+            return carry
+
+        lax.fori_loop(0, ff // tile, sums, 0)
+
+        def sums_down(step, carry):
+            col = pl.ds(pl.multiple_of(step * tile, tile), tile)
+            put(gd_ref, col, dot(hs_s[all_rows, :], og_s[all_rows, col], tn))
+            return carry
+
+        lax.fori_loop(0, width // tile, sums_down, 0)
 
     @pl.when(phase == 0)
     def _():
-        own = pl.ds(pl.multiple_of(core * queue, queue), queue)
+        work(1, 0)
+        own = pl.ds(0, queue)
 
         def returns(step, carry):
             col = pl.ds(pl.multiple_of(step * tile, tile), tile)
@@ -260,45 +311,28 @@
 
         lax.fori_loop(0, width // tile, returns, 0)
 
-    @pl.when((phase == 0) & (expert == exp_local - 1))
-    def _():
-        for which, acc in enumerate((out_acc, gtok_acc)):
-            stage_s[which] = acc[...].astype(bf16).reshape(peers, rows, width)
-            for offset in range(1, peers):
-                back(which, offset).start()
-
-    wide, narrow = width // reps, ff // reps
-    for rep in range(reps):
-        @pl.when(rep_me == rep)
+        @pl.when(expert == exp_local - 1)
         def _():
-            xs_s[...] = x_s[:, rep * wide:(rep + 1) * wide]
-            hs_s[...] = h_s[:, rep * narrow:(rep + 1) * narrow]
-
-    @pl.when(phase == 0)
-    def _():
-        gg_ref[expert] = jnp.zeros((wide, ff), f32)
-        gu_ref[expert] = jnp.zeros((wide, ff), f32)
-        gd_ref[expert] = jnp.zeros((narrow, width), f32)
-
-    def sums(step, carry):
-        col = pl.ds(pl.multiple_of(step * tile, tile), tile)
-        gg_ref[expert, :, col] += dot(xs_s[...], gb_s[:, col], tn)
-        gu_ref[expert, :, col] += dot(xs_s[...], ub_s[:, col], tn)
-        return carry
-
-    lax.fori_loop(0, ff // tile, sums, 0)
-
-    def sums_down(step, carry):
-        col = pl.ds(pl.multiple_of(step * tile, tile), tile)
-        gd_ref[expert, :, col] += dot(hs_s[...], og_s[:, col], tn)
-        return carry
-
-    lax.fori_loop(0, width // tile, sums_down, 0)
+            for which, acc in enumerate((out_acc, gtok_acc)):
+                stage_s[which] = acc[...].astype(bf16).reshape(peers, rows, width)
+                for offset in range(1, peers):
+                    back(which, offset).start()
+
+        total(1, True)
+
+        @pl.when(expert == exp_local - 1)
+        def _():
+            relay(1)
+
+    @pl.when(phase == 1)
+    def _():
+        work(reps - 1, 1)
+        total(reps - 1, False)
 
     @pl.when((phase == 1) & (expert == exp_local - 1))
     def _():
         for which, (acc, ref) in enumerate(((out_acc, out_ref), (gtok_acc, gtok_ref))):
-            total = acc[pl.ds(pl.multiple_of(me * rows, rows), rows), :]
+            added = acc[pl.ds(pl.multiple_of(me * rows, rows), rows), :]
             for offset in range(1, peers):
                 where = lax.rem(me + peers - offset, peers)
                 pltpu.make_async_remote_copy(
@@ -309,12 +343,20 @@
                     device_id={"dp": mate},
                     device_id_type=MESH,
                 ).wait_recv()
-                total = total + land_s[which, where].astype(f32)
-            ref[...] = total.astype(bf16)
+                added = added + land_s[which, where].astype(f32)
+            ref[...] = added.astype(bf16)
         for which in range(2):
             for offset in range(1, peers):
                 back(which, offset).wait_send()
-            for place in range(4 * peers - 1):
+            for distance in range(peers - 1):
+                @pl.when((me >= distance) & (me < peers - 1))
+                def _():
+                    along(which, me, distance, 1).wait_send()
+
+                @pl.when((me + distance < peers) & (me > 0))
+                def _():
+                    along(which, me, distance, -1).wait_send()
+            for place in range(2 * peers - 2, 5 * peers - 2):
                 push(which, me, rep_me, place, {"dp": mate}).wait_send()
 
 
@@ -332,7 +374,7 @@
     gates = jnp.sum(jnp.where(chosen, gate_values[:, :, None].astype(f32), 0.0), axis=1).astype(bf16)
     packed = jnp.concatenate([tokens, gates], axis=1)
     sizes = (peers, reps, rows, width, ff, exp_local, queue)
-    group, every = peers * rows, 2 * queue
+    group, every = peers * rows, (reps - 1) * queue
     wide, narrow = width // reps, ff // reps
     whole = lambda *shape: pl.BlockSpec(shape, lambda p, e: (0,) * len(shape), pipeline_mode=pl.Buffered(1))
     each = lambda a, b: pl.BlockSpec((1, a, b), lambda p, e: (e, 0, 0))
@@ -344,8 +386,8 @@
         scratch_shapes=[
             pltpu.VMEM((peers, reps, rows, width + lanes), bf16),
             pltpu.VMEM((peers, reps, rows, width), bf16),
-            pltpu.VMEM((2, lanes, group), f32),
-            pltpu.VMEM((2, lanes, group), f32),
+            pltpu.VMEM((reps - 1, lanes, group), f32),
+            pltpu.VMEM((reps - 1, lanes, group), f32),
             pltpu.VMEM((every, width), bf16),
             pltpu.VMEM((every, width), bf16),
             pltpu.VMEM((every, ff), bf16),
@@ -359,7 +401,7 @@
             pltpu.VMEM((group, width), f32),
             pltpu.VMEM((2, peers, rows, width), bf16),
             pltpu.VMEM((2, peers, rows, width), bf16),
-            pltpu.SemaphoreType.DMA((2, 4 * peers - 1)),
+            pltpu.SemaphoreType.DMA((2, 5 * peers - 2)),
             pltpu.SemaphoreType.DMA((2, peers, reps)),
             pltpu.SemaphoreType.DMA((2, peers - 1)),
             pltpu.SemaphoreType.DMA((2, peers)),

time: 195 us -> 159 us (0.82)
  Pallas kernels: 174 us -> 139 us
    pallas_call x1, Pallas kernels: 174 us -> 139 us  [fused_shards(): pl.pallas_call(functools.partial(fused_kernel, sizes), grid=(2, exp_local...]
where the time goes in v3:
time: 159 us; the launch traced here: 157 us
  Pallas kernels  139 us (87%)
  local copies, waits for them, and re-layouts  13.4 us (8%)
  other arithmetic  3.37 us (2%)
    pallas_call x1, Pallas kernels, fused_shards(): pl.pallas_call(functools.partial(fused_kernel, sizes), grid=(2, exp_local...  139 us
    unnamed x9, local copies, waits for them, and re-layouts  13.4 us

profile of v3, /device:TPU:0, one launch (start us, length us, event | category | flops | bytes accessed | tf_op | source)
XLA Modules:
  0.0 156.8 jit_solution(5576781086782805515)
XLA Ops:
  0.6 0.7 convert_element_type.7
  1.3 1.0 select_reduce_fusion
  2.3 1.7 %pad_maximum_fusion.tok_ref = bf16[128,1408]{1,0:T(8,128)(2,1)} fusion(bf16[128,128]{1,0:T(8,128)(2,1)S(1)} %select_reduce_fusion, bf16[128,1280]{1,0:T(8,128)(2,1)} %param.7), kind=kLoop, calls=%fused_computation.2 | loop fusion | flops 720896 | bytes 720896 | tf_op jit(solution)/shard_map/concatenate | solution.py:375
  4.0 139.3 %shard_map.110 = (bf16[128,1280]{1,0:T(8,128)(2,1)}, bf16[128,1280]{1,0:T(8,128)(2,1)}, f32[4,320,768]{2,1,0:T(8,128)}, f32[4,320,768]{2,1,0:T(8,128)}, f32[4,192,1280]{2,1,0:T(8,128)}) custom-call(bf16[128,1408]{1,0:T(8,128)(2,1)} %pad_maximum_fusion.tok_ref, bf16[128,1280]{1,0:T(8,128)(2,1)} %cot_ref.1, bf16[4,1280,768]{2,1,0:T(8,128)(2,1)} %wg_ref.1, ...), custom_call_target="tpu_custom_call" | custom-call | tf_op jit(solution)/shard_map/pallas_call | solution.py:381
  143.3 1.7 %copy.19 = bf16[128,1280]{1,0:T(8,128)(2,1)} copy(bf16[128,1280]{1,0:T(8,128)(2,1)} %get-tuple-element.10) | data formatting | bytes 655360
  145.1 1.7 %copy.20 = bf16[128,1280]{1,0:T(8,128)(2,1)} copy(bf16[128,1280]{1,0:T(8,128)(2,1)} %get-tuple-element.11) | data formatting | bytes 655360
  146.8 0.0 copy-start.1
  146.8 4.6 %copy.21 = f32[4,320,768]{2,1,0:T(8,128)} copy(f32[4,320,768]{2,1,0:T(8,128)} %get-tuple-element.12) | data formatting | bytes 7864320
  151.3 0.0 copy-done.1
  151.3 0.0 copy-start
  151.3 2.0 %copy.22 = f32[4,320,768]{2,1,0:T(8,128)} copy(f32[4,320,768]{2,1,0:T(8,128)S(1)} %copy-done.1) | data formatting | bytes 7864320
  153.4 1.5 copy-done
  154.9 1.9 %copy.23 = f32[4,192,1280]{2,1,0:T(8,128)} copy(f32[4,192,1280]{2,1,0:T(8,128)S(1)} %copy-done) | data formatting | bytes 7864320
Async XLA Ops:
  146.8 4.6 %copy-start.1 = (f32[4,320,768]{2,1,0:T(8,128)S(1)}, f32[4,320,768]{2,1,0:T(8,128)}, u32[]{:S(2)}) copy-start(f32[4,320,768]{2,1,0:T(8,128)} %get-tuple-element.13) | copy-start | bytes 11796484
  151.3 3.5 %copy-start = (f32[4,192,1280]{2,1,0:T(8,128)S(1)}, f32[4,192,1280]{2,1,0:T(8,128)}, u32[]{:S(2)}) copy-start(f32[4,192,1280]{2,1,0:T(8,128)} %get-tuple-element.14) | copy-start | bytes 11796484

commit v4 on v3

--- a/solution.py
+++ b/solution.py
@@ -305,18 +305,27 @@
             col = pl.ds(pl.multiple_of(step * tile, tile), tile)
             expert_out = dot(h_s[own, :], wd_ref[0, :, col], nn).astype(bf16)
             out_acc[:, col] += dot(pg_s[...], expert_out, tn)
-            slot_grad = (dot(gb_s[own, :], wg_ref[0, col, :], nt) + dot(ub_s[own, :], wu_ref[0, col, :], nt)).astype(bf16)
-            gtok_acc[:, col] += dot(p_s[...], slot_grad, tn)
             return carry
 
         lax.fori_loop(0, width // tile, returns, 0)
 
-        @pl.when(expert == exp_local - 1)
-        def _():
-            for which, acc in enumerate((out_acc, gtok_acc)):
+        def send_back(which, acc):
+            @pl.when(expert == exp_local - 1)
+            def _():
                 stage_s[which] = acc[...].astype(bf16).reshape(peers, rows, width)
                 for offset in range(1, peers):
                     back(which, offset).start()
+
+        send_back(0, out_acc)
+
+        def returns_grad(step, carry):
+            col = pl.ds(pl.multiple_of(step * tile, tile), tile)
+            slot_grad = (dot(gb_s[own, :], wg_ref[0, col, :], nt) + dot(ub_s[own, :], wu_ref[0, col, :], nt)).astype(bf16)
+            gtok_acc[:, col] += dot(p_s[...], slot_grad, tn)
+            return carry
+
+        lax.fori_loop(0, width // tile, returns_grad, 0)
+        send_back(1, gtok_acc)
 
         total(1, True)
 

time: 159 us -> 167 us (1.050)
  Pallas kernels: 139 us -> 148 us
    pallas_call x1, Pallas kernels: 139 us -> 148 us  [fused_shards(): pl.pallas_call(functools.partial(fused_kernel, sizes), grid=(2, exp_local...]
where the time goes in v4:
time: 167 us; the launch traced here: 165 us
  Pallas kernels  148 us (89%)
  local copies, waits for them, and re-layouts  13.4 us (8%)
  other arithmetic  3.37 us (2%)
    pallas_call x1, Pallas kernels, fused_shards(): pl.pallas_call(functools.partial(fused_kernel, sizes), grid=(2, exp_local...  148 us
    unnamed x9, local copies, waits for them, and re-layouts  13.4 us

profile of v4, /device:TPU:0, one launch (start us, length us, event | category | flops | bytes accessed | tf_op | source)
XLA Modules:
  0.0 165.4 jit_solution(5335143043709412431)
XLA Ops:
  0.6 0.7 convert_element_type.7
  1.3 1.0 select_reduce_fusion
  2.3 1.7 %pad_maximum_fusion.tok_ref = bf16[128,1408]{1,0:T(8,128)(2,1)} fusion(bf16[128,128]{1,0:T(8,128)(2,1)S(1)} %select_reduce_fusion, bf16[128,1280]{1,0:T(8,128)(2,1)} %param.7), kind=kLoop, calls=%fused_computation.2 | loop fusion | flops 720896 | bytes 720896 | tf_op jit(solution)/shard_map/concatenate | solution.py:384
  4.0 147.9 %shard_map.110 = (bf16[128,1280]{1,0:T(8,128)(2,1)}, bf16[128,1280]{1,0:T(8,128)(2,1)}, f32[4,320,768]{2,1,0:T(8,128)}, f32[4,320,768]{2,1,0:T(8,128)}, f32[4,192,1280]{2,1,0:T(8,128)}) custom-call(bf16[128,1408]{1,0:T(8,128)(2,1)} %pad_maximum_fusion.tok_ref, bf16[128,1280]{1,0:T(8,128)(2,1)} %cot_ref.1, bf16[4,1280,768]{2,1,0:T(8,128)(2,1)} %wg_ref.1, ...), custom_call_target="tpu_custom_call" | custom-call | tf_op jit(solution)/shard_map/pallas_call | solution.py:390
  151.9 1.7 %copy.19 = bf16[128,1280]{1,0:T(8,128)(2,1)} copy(bf16[128,1280]{1,0:T(8,128)(2,1)} %get-tuple-element.10) | data formatting | bytes 655360
  153.6 1.7 %copy.20 = bf16[128,1280]{1,0:T(8,128)(2,1)} copy(bf16[128,1280]{1,0:T(8,128)(2,1)} %get-tuple-element.11) | data formatting | bytes 655360
  155.3 0.0 copy-start.1
  155.3 4.6 %copy.21 = f32[4,320,768]{2,1,0:T(8,128)} copy(f32[4,320,768]{2,1,0:T(8,128)} %get-tuple-element.12) | data formatting | bytes 7864320
  159.9 0.0 copy-done.1
  159.9 0.0 copy-start
  159.9 2.0 %copy.22 = f32[4,320,768]{2,1,0:T(8,128)} copy(f32[4,320,768]{2,1,0:T(8,128)S(1)} %copy-done.1) | data formatting | bytes 7864320
  161.9 1.5 copy-done
  163.4 1.9 %copy.23 = f32[4,192,1280]{2,1,0:T(8,128)} copy(f32[4,192,1280]{2,1,0:T(8,128)S(1)} %copy-done) | data formatting | bytes 7864320
Async XLA Ops:
  155.3 4.6 %copy-start.1 = (f32[4,320,768]{2,1,0:T(8,128)S(1)}, f32[4,320,768]{2,1,0:T(8,128)}, u32[]{:S(2)}) copy-start(f32[4,320,768]{2,1,0:T(8,128)} %get-tuple-element.13) | copy-start | bytes 11796484
  159.9 3.5 %copy-start = (f32[4,192,1280]{2,1,0:T(8,128)S(1)}, f32[4,192,1280]{2,1,0:T(8,128)}, u32[]{:S(2)}) copy-start(f32[4,192,1280]{2,1,0:T(8,128)} %get-tuple-element.14) | copy-start | bytes 11796484
